TPU v7x, 32 devices: a whole 2x2x4 slice. The times are simulated.
32 devices in a mesh: dp: 16 (over z, y, core), ctx: 2 (over x).
Axes of the slice: x: 2, y: 2, z: 4, core: 2. Of those that a mesh axis runs over, the one named last changes fastest.
Arguments:
- conv_input: bfloat16 [16, 256, 4096], P('dp', 'ctx'), may hold values from -6 to 6
- gate_value: bfloat16 [16, 256, 4096], P('dp', 'ctx'), may hold values from -6 to 6
- out_grad: bfloat16 [16, 256, 4096], P('dp', 'ctx'), may hold values from -6 to 6
- filter_taps: bfloat16 [128, 4096], P('dp'), may hold values from -0.5 to 0.5
Outputs:
- input_grad: bfloat16 [16, 256, 4096], P('dp', 'ctx')
- filter_grad: float32 [128, 4096], P('dp')
All inputs are finite; a program needn't handle non-finite values.
Results may differ from a plain program's by a relative error of at most 0.0051.
Values may be sent and summed in bfloat16 or wider, within the bound.
A program may use at most 64 MiB of HBM per device.

v0:
```python
import math
import jax
import jax.numpy as jnp
import numpy as np
from jax import lax
from jax.sharding import PartitionSpec as P


def split(values):
    high = values.astype(jnp.bfloat16)
    return (high, (values - high.astype(np.float32)).astype(jnp.bfloat16))


def transforms(length):
    half = length // 2
    angle = np.pi * np.outer(2 * np.arange(half) + 1, np.arange(length)) / length
    forward = np.concatenate([np.cos(angle), -np.sin(angle)], 0)
    inverse = np.concatenate([np.cos(angle), -np.sin(angle)], 0).T / half
    return (split(forward.astype(np.float32)), split(inverse.astype(np.float32)))


def dot(a, b):
    return lax.dot_general(a, b, (((1,), (0,)), ((), ())), preferred_element_type=jnp.float32)


def shards(conv_input, gate_value, out_grad, filter_taps):
    inputs = conv_input[0]
    rows = inputs.shape[0]
    taps = filter_taps.shape[0] * lax.axis_size("dp")
    (fh, fl), (bh, bl) = transforms(rows + taps)
    half = (rows + taps) // 2
    mixed = (out_grad[0].astype(jnp.float32) * gate_value[0].astype(jnp.float32)).astype(
        jnp.bfloat16
    )
    devices = lax.axis_size("ctx")
    rim = lax.ppermute(mixed[:taps], "ctx", [(i + 1, i) for i in range(devices - 1)])
    full_taps = lax.all_gather(filter_taps, "dp", axis=0, tiled=True)

    def spectrum(x, first=0):
        n = x.shape[0]
        s = dot(fh[:, first : first + n], x) + dot(fl[:, first : first + n], x)
        return (s[:half], s[half:])

    def back(re, im, n):
        s = jnp.concatenate([re, im], 0)
        high = s.astype(jnp.bfloat16)
        low = (s - high.astype(jnp.float32)).astype(jnp.bfloat16)
        return dot(bh[:n], high) + dot(bl[:n], high) + dot(bh[:n], low)

    xr, xi = spectrum(inputs)
    gr0, gi0 = spectrum(mixed)
    gr1, gi1 = spectrum(rim, rows)
    gr, gi = (gr0 + gr1, gi0 + gi1)
    partial = back(xr * gr + xi * gi, xr * gi - xi * gr, taps)
    hr, hi = spectrum(full_taps)
    grad = back(hr * gr + hi * gi, hr * gi - hi * gr, rows)
    shard_grad = lax.psum(lax.psum_scatter(partial, "dp", scatter_dimension=0, tiled=True), "ctx")
    tokens_all = rows * devices * lax.axis_size("dp")
    return (grad.astype(jnp.bfloat16)[None], shard_grad * (1.0 / math.sqrt(tokens_all)))


def solution(mesh):
    in_specs = (P("dp", "ctx", None), P("dp", "ctx", None), P("dp", "ctx", None), P("dp", None))
    out_specs = (P("dp", "ctx", None), P("dp", None))
    return jax.shard_map(shards, mesh=mesh, in_specs=in_specs, out_specs=out_specs, check_vma=False)
```

profile of v0, /device:TPU:0, one launch (start us, length us, event | category | flops | bytes accessed | tf_op | source)
XLA Modules:
  0.0 203.6 jit_solution(12447030233872739120)
XLA Ops:
  7.2 0.0 copy-start
  7.2 0.0 copy-start.10
  7.2 0.0 all-gather.2.cloned.1.call-start
  7.2 1.9 fusion.7
  9.1 1.3 collective-permute-start
  10.4 0.0 all-gather.2.cloned.1.call-update
  10.4 0.0 reduce-scatter.4.cloned.1.call-start
  10.5 0.0 copy-done.10
  10.5 0.7 fusion.26
  11.2 0.0 copy-done
  11.2 0.0 copy-start.9
  11.2 0.7 fusion.9
  11.9 0.1 copy-done.9
  12.0 0.7 fusion.1
  12.8 0.0 copy-start.13
  12.8 0.7 convolution_add_fusion.2
  13.5 0.0 copy-start.2
  13.6 0.0 copy-start.12
  13.6 23.0 %collective-permute-done = bf16[128,4096]{1,0:T(8,128)(2,1)S(1)} collective-permute-done((bf16[128,4096]{1,0:T(8,128)(2,1)S(1)}, bf16[128,4096]{1,0:T(8,128)(2,1)S(1)}, u32[]{:S(2)}, u32[]{:S(2)}) %collective-permute-start) | collective-permute-done | bytes 1048608 | tf_op jit(solution)/shard_map/ppermute | solution.py:36
  36.6 0.0 copy-done.13
  36.6 0.7 fusion.27
  37.3 0.0 copy-done.12
  37.3 0.7 fusion
  38.0 0.0 copy-done.2
  38.0 3.2 %multiply_add_fusion = (f32[128,4096]{1,0:T(8,128)}, f32[128,4096]{1,0:T(8,128)}, f32[128,4096]{1,0:T(8,128)}) fusion(f32[256,4096]{1,0:T(8,128)S(1)} %convolution_add_fusion.2, f32[256,4096]{1,0:T(8,128)S(1)} %fusion, f32[256,4096]{1,0:T(8,128)S(1)} %fusion.1), kind=kLoop, calls=%fused_computation.22 | loop fusion | flops 2621440 | bytes 18874368 | tf_op jit(solution)/shard_map/add | solution.py:54
  41.2 11.2 %all-gather.2.cloned.1.call-done = bf16[128,4096]{1,0:T(8,128)(2,1)} async-done(((bf16[8,4096]{1,0:T(8,128)(2,1)}), bf16[128,4096]{1,0:T(8,128)(2,1)}) %all-gather.2.cloned.1.call-update) | async-done | bytes 1048592 | tf_op jit(solution)/shard_map/all_gather | solution.py:37
  52.4 0.0 copy-start.7
  52.4 2.0 fusion.25
  54.4 0.0 copy-done.7
  54.4 0.0 copy-start.3
  54.4 0.0 copy-start.6
  54.4 0.7 convolution_add_fusion.3
  55.2 1.4 copy-done.3
  56.6 0.7 copy-done.6
  57.3 0.0 copy-start.5
  57.3 0.0 copy-start.8
  57.3 4.2 %multiply_add_fusion.1 = (f32[128,4096]{1,0:T(8,128)S(1)}, f32[128,4096]{1,0:T(8,128)}, f32[128,4096]{1,0:T(8,128)S(1)}) fusion(f32[128,4096]{1,0:T(8,128)S(1)} %copy-done.6, f32[128,4096]{1,0:T(8,128)} %get-tuple-element.8, f32[256,4096]{1,0:T(8,128)S(1)} %convolution_add_fusion.3, f32[256,4096]{1,0:T(8,128)S(1)} %copy-done.3), kind=kLoop, calls=%fused_computation.24 | loop fusion | flops 4718592 | bytes 18874368 | tf_op jit(solution)/shard_map/add | solution.py:56
  61.5 0.0 copy-done.5
  61.5 0.0 copy-done.8
  61.5 0.0 copy-start.11
  61.5 0.8 fusion.17
  62.3 0.1 copy-done.11
  62.3 0.8 convolution_add_fusion.5
  63.1 2.1 %fusion.2 = f32[128,4096]{0,1:T(8,128)} fusion(f32[4096,128]{1,0:T(8,128)S(1)} %convolution_add_fusion.5, bf16[128,256]{1,0:T(8,128)(2,1)S(1)} %copy-done.8, f32[128,4096]{1,0:T(8,128)S(1)} %get-tuple-element.11, f32[128,4096]{1,0:T(8,128)S(1)} %copy-done.5), kind=kOutput, calls=%fused_computation.7 | convolution fusion | flops 274202624 | bytes 8454144 | tf_op jit(solution)/shard_map/dot_general | solution.py:23
  65.2 3.0 %copy.24 = f32[128,4096]{1,0:T(8,128)} copy(f32[128,4096]{0,1:T(8,128)} %fusion.2) | data formatting | bytes 4194304
  68.1 0.0 reduce-scatter.4.cloned.1.call-update
  68.2 0.2 all-reduce.2.cloned.1.call-start
  68.4 0.0 copy-start.4
  68.4 2.5 %fusion.13 = f32[4096,128]{1,0:T(8,128)S(1)} fusion(bf16[128,256]{1,0:T(8,128)(2,1)S(1)} %copy-done.8, f32[128,4096]{1,0:T(8,128)} %get-tuple-element.10, f32[128,4096]{1,0:T(8,128)S(1)} %get-tuple-element.9), kind=kOutput, calls=%fused_computation.31 | convolution fusion | flops 272629760 | bytes 6356992 | tf_op jit(solution)/shard_map/dot_general | solution.py:23
  70.9 0.0 copy-done.4
  70.9 2.1 %convolution_add_fusion.7 = f32[4096,128]{1,0:T(8,128)} fusion(f32[4096,128]{1,0:T(8,128)S(1)} %fusion.13, bf16[128,256]{1,0:T(8,128)(2,1)S(1)} %copy-done.11, f32[128,4096]{1,0:T(8,128)S(1)} %copy-done.4, f32[128,4096]{1,0:T(8,128)S(1)} %get-tuple-element.9), kind=kOutput, calls=%fused_computation.10 | convolution fusion | flops 273154048 | bytes 8454144 | tf_op jit(solution)/shard_map/dot_general | solution.py:23
  73.0 56.1 %reduce-scatter.4.cloned.1.call-done = f32[8,4096]{1,0:T(8,128)} async-done(((f32[128,4096]{1,0:T(8,128)}), f32[8,4096]{1,0:T(8,128)}) %reduce-scatter.4.cloned.1.call-update) | async-done | bytes 131088
  129.1 2.9 %copy.25 = f32[8,4096]{0,1:T(8,128)} copy(f32[8,4096]{1,0:T(8,128)} %reduce-scatter.4.cloned.1.call-done) | data formatting | bytes 262144
  132.0 0.0 all-reduce.2.cloned.1.call-update
  132.0 3.0 %fusion.4 = bf16[1,128,4096]{1,2,0:T(8,128)(2,1)S(1)} fusion(f32[4096,128]{1,0:T(8,128)} %convolution_add_fusion.7, bf16[128,256]{1,0:T(8,128)(2,1)S(1)} %copy-done.8, f32[128,4096]{1,0:T(8,128)} %get-tuple-element.10, f32[128,4096]{1,0:T(8,128)S(1)} %get-tuple-element.9), kind=kOutput, calls=%fused_computation.12 | convolution fusion | flops 274726912 | bytes 7405568 | tf_op jit(solution)/shard_map/dot_general | solution.py:23
  135.0 1.3 copy.22
  136.3 57.7 %all-reduce.2.cloned.1.call-done = f32[8,4096]{0,1:T(8,128)} async-done(((f32[8,4096]{0,1:T(8,128)}), f32[8,4096]{0,1:T(8,128)}) %all-reduce.2.cloned.1.call-update) | async-done | bytes 131088 | tf_op jit(solution)/shard_map/psum | solution.py:57
  194.0 0.0 copy-start.1
  194.0 1.8 broadcast_multiply_fusion
  195.8 1.2 copy.23
  197.1 0.0 copy-done.1
Async XLA Ops:
  7.2 4.0 %copy-start = (bf16[1,128,4096]{2,1,0:T(8,128)(2,1)S(1)}, bf16[1,128,4096]{2,1,0:T(8,128)(2,1)}, u32[]{:S(2)}) copy-start(bf16[1,128,4096]{2,1,0:T(8,128)(2,1)} %param.18) | copy-start | bytes 3145732
  7.2 3.3 %copy-start.10 = (bf16[256,128]{1,0:T(8,128)(2,1)S(1)}, bf16[256,128]{1,0:T(8,128)(2,1)}, u32[]{:S(2)}) copy-start(bf16[256,128]{1,0:T(8,128)(2,1)} %constant.14.clone) | copy-start | bytes 196612
  7.2 45.2 %all-gather.2.cloned.1.call-start = ((), (), s32[]{:S(2)}) async-start(), calls=%async_computation.1 | async-start | bytes 1114112 | tf_op jit(solution)/shard_map/all_gather | solution.py:37
  9.1 27.5 %collective-permute-start = (bf16[128,4096]{1,0:T(8,128)(2,1)S(1)}, bf16[128,4096]{1,0:T(8,128)(2,1)S(1)}, u32[]{:S(2)}, u32[]{:S(2)}) collective-permute-start(bf16[128,4096]{1,0:T(8,128)(2,1)S(1)} %fusion.7), channel_id=1, source_target_pairs={{1,0},{3,2},{5,4},{7,6},{9,8},{11,10},{13,12},{15,14},{17,16},{19,... | collective-permute-start | bytes 3145736 | tf_op jit(solution)/shard_map/ppermute | solution.py:36
  10.4 118.7 %reduce-scatter.4.cloned.1.call-start = ((), (), s32[]{:S(2)}) async-start(), calls=%async_computation.3 | async-start | bytes 2228224
  11.2 0.8 copy-start.9
  12.8 23.8 %copy-start.13 = (bf16[256,128]{1,0:T(8,128)(2,1)S(1)}, bf16[256,128]{1,0:T(8,128)(2,1)}, u32[]{:S(2)}) copy-start(bf16[256,128]{1,0:T(8,128)(2,1)} %constant.17.clone) | copy-start | bytes 196612
  13.5 24.5 %copy-start.2 = (f32[256,4096]{1,0:T(8,128)}, f32[256,4096]{1,0:T(8,128)S(1)}, u32[]{:S(2)}) copy-start(f32[256,4096]{1,0:T(8,128)S(1)} %convolution_add_fusion.2) | copy-start | bytes 12582916
  13.6 23.7 %copy-start.12 = (bf16[256,128]{1,0:T(8,128)(2,1)S(1)}, bf16[256,128]{1,0:T(8,128)(2,1)}, u32[]{:S(2)}) copy-start(bf16[256,128]{1,0:T(8,128)(2,1)} %constant.16.clone) | copy-start | bytes 196612
  52.4 2.0 copy-start.7
  54.4 2.2 %copy-start.3 = (f32[256,4096]{1,0:T(8,128)S(1)}, f32[256,4096]{1,0:T(8,128)}, u32[]{:S(2)}) copy-start(f32[256,4096]{1,0:T(8,128)} %copy-done.2) | copy-start | bytes 12582916
  54.4 2.9 %copy-start.6 = (f32[128,4096]{1,0:T(8,128)S(1)}, f32[128,4096]{1,0:T(8,128)}, u32[]{:S(2)}) copy-start(f32[128,4096]{1,0:T(8,128)} %get-tuple-element.7) | copy-start | bytes 6291460
  57.3 4.2 %copy-start.5 = (f32[128,4096]{1,0:T(8,128)S(1)}, f32[128,4096]{1,0:T(8,128)}, u32[]{:S(2)}) copy-start(f32[128,4096]{1,0:T(8,128)} %get-tuple-element.6) | copy-start | bytes 6291460
  57.3 4.2 %copy-start.8 = (bf16[128,256]{1,0:T(8,128)(2,1)S(1)}, bf16[128,256]{1,0:T(8,128)(2,1)}, u32[]{:S(2)}) copy-start(bf16[128,256]{1,0:T(8,128)(2,1)} %constant.18.clone) | copy-start | bytes 196612
  61.5 0.8 copy-start.11
  68.2 125.9 %all-reduce.2.cloned.1.call-start = ((), (), s32[]{:S(2)}) async-start(), calls=%async_computation.2 | async-start | bytes 4194304 | tf_op jit(solution)/shard_map/psum | solution.py:57
  68.4 2.5 %copy-start.4 = (f32[128,4096]{1,0:T(8,128)S(1)}, f32[128,4096]{1,0:T(8,128)}, u32[]{:S(2)}) copy-start(f32[128,4096]{1,0:T(8,128)} %get-tuple-element.10) | copy-start | bytes 6291460
  194.0 3.1 %copy-start.1 = (bf16[1,128,4096]{2,1,0:T(8,128)(2,1)S(1)}, bf16[1,128,4096]{2,1,0:T(8,128)(2,1)}, u32[]{:S(2)}) copy-start(bf16[1,128,4096]{2,1,0:T(8,128)(2,1)} %param.18) | copy-start | bytes 3145732
Sparse Core Ops, SparseCore 0:
  10.6 41.7 all-gather.1
  68.3 60.7 reduce-scatter.3
  132.1 61.8 all-reduce.1
where the time goes:
time: 204 us
  waiting for transfers between devices  148 us (73%)
  matrix products  18.2 us (9%)
  between operations  14 us (7%)
  other arithmetic  11.1 us (5%)
  local copies, waits for them, and re-layouts  10.7 us (5%)
    psum x1, waiting for transfers between devices, shards(): lax.psum(lax.psum_scatter(partial, 'dp', scatter_dimension=0, tiled=True)...  57.7 us
    unnamed x4, waiting for transfers between devices  56.1 us
    ppermute x1, waiting for transfers between devices, shards(): lax.ppermute(mixed[:taps], 'ctx', [(i + 1, i) for i in range(devices - 1)])  23 us
    dot_general x14, matrix products, dot(): lax.dot_general(a, b, (((1,), (0,)), ((), ())), preferred_element_type=jn...  18.2 us
    all_gather x1, waiting for transfers between devices, shards(): full_taps = lax.all_gather(filter_taps, 'dp', axis=0, tiled=True)  11.2 us
    unnamed x32, local copies, waits for them, and re-layouts  10.7 us
    add x1, other arithmetic, shards(): grad = back(hr * gr + hi * gi, hr * gi - hi * gr, rows)  4.21 us
  transfers between devices with their start and end apart: 4, of which 4 were waited for; matrix products, arithmetic and copies ran while one was open for 8% of the time, Pallas kernels for 0%

commit v1 on v0

--- a/solution.py
+++ b/solution.py
@@ -54,7 +54,10 @@
     partial = back(xr * gr + xi * gi, xr * gi - xi * gr, taps)
     hr, hi = spectrum(full_taps)
     grad = back(hr * gr + hi * gi, hr * gi - hi * gr, rows)
-    shard_grad = lax.psum(lax.psum_scatter(partial, "dp", scatter_dimension=0, tiled=True), "ctx")
+    shard_grad = jnp.sum(
+        lax.all_gather(lax.psum_scatter(partial, "dp", scatter_dimension=0, tiled=True), "ctx"),
+        axis=0,
+    )
     tokens_all = rows * devices * lax.axis_size("dp")
     return (grad.astype(jnp.bfloat16)[None], shard_grad * (1.0 / math.sqrt(tokens_all)))
 

time: 204 us -> 143 us (0.70)
  waiting for transfers between devices: 148 us -> 87.7 us
  blocking collectives: 0 us -> 5.83 us
  local copies, waits for them, and re-layouts: 10.7 us -> 7.59 us
  matrix products: 18.2 us -> 15.7 us
    psum x1 -> x0, waiting for transfers between devices: 57.7 us -> none  [shards(): lax.psum(lax.psum_scatter(partial, 'dp', scatter_dimension=0, tiled=True)...]
    unnamed x4 -> x2, waiting for transfers between devices: 56.1 us -> 0.03 us
    reduce_scatter x0 -> x1, waiting for transfers between devices: none -> 53.6 us  [shards(): lax.psum_scatter(partial, 'dp', scatter_dimension=0, tiled=True)]
    all_gather x0 -> x1, blocking collectives: none -> 5.83 us  [shards(): lax.all_gather(lax.psum_scatter(partial, 'dp', scatter_dimension=0, tiled...]
    unnamed x32 -> x30, local copies, waits for them, and re-layouts: 10.7 us -> 7.59 us
    dot_general x14, matrix products: 18.2 us -> 15.7 us  [dot(): lax.dot_general(a, b, (((1,), (0,)), ((), ())), preferred_element_type=jn...]
  transfers between devices with their start and end apart: 4 -> 3, of which waited for: 4 -> 3; matrix products, arithmetic and copies ran while one was open for 8% -> 10% of each run, Pallas kernels for 0% -> 0%
where the time goes in v1:
time: 143 us; the launch traced here: 142 us
  waiting for transfers between devices  87.7 us (61%)
  matrix products  15.7 us (11%)
  between operations  14.3 us (10%)
  other arithmetic  9.98 us (7%)
  local copies, waits for them, and re-layouts  7.59 us (5%)
  blocking collectives  5.83 us (4%)
    reduce_scatter x1, waiting for transfers between devices, shards(): lax.psum_scatter(partial, 'dp', scatter_dimension=0, tiled=True)  53.6 us
    ppermute x1, waiting for transfers between devices, shards(): lax.ppermute(mixed[:taps], 'ctx', [(i + 1, i) for i in range(devices - 1)])  23 us
    dot_general x14, matrix products, dot(): lax.dot_general(a, b, (((1,), (0,)), ((), ())), preferred_element_type=jn...  15.7 us
    all_gather x1, waiting for transfers between devices, shards(): full_taps = lax.all_gather(filter_taps, 'dp', axis=0, tiled=True)  11.1 us
    unnamed x30, local copies, waits for them, and re-layouts  7.59 us
    all_gather x1, blocking collectives, shards(): lax.all_gather(lax.psum_scatter(partial, 'dp', scatter_dimension=0, tiled...  5.83 us
    add x1, other arithmetic, shards(): grad = back(hr * gr + hi * gi, hr * gi - hi * gr, rows)  4.21 us
    add x1, other arithmetic, shards(): partial = back(xr * gr + xi * gi, xr * gi - xi * gr, taps)  3.22 us
  transfers between devices with their start and end apart: 3, of which 3 were waited for; matrix products, arithmetic and copies ran while one was open for 10% of the time, Pallas kernels for 0%

profile of v1, /device:TPU:0, one launch (start us, length us, event | category | flops | bytes accessed | tf_op | source)
XLA Modules:
  0.0 142.5 jit_solution(1577224262711718549)
XLA Ops:
  7.2 0.0 copy-start
  7.2 0.0 copy-start.10
  7.2 0.0 all-gather.3.cloned.1.call-start
  7.2 1.9 %fusion.7 = bf16[128,4096]{1,0:T(8,128)(2,1)S(1)} fusion(bf16[1,128,4096]{2,1,0:T(8,128)(2,1)} %param.19, bf16[1,128,4096]{2,1,0:T(8,128)(2,1)} %param.20), kind=kLoop, calls=%fused_computation.26 | loop fusion | flops 2097152 | bytes 3145728 | tf_op jit(solution)/shard_map/convert_element_type | solution.py:32
  9.1 1.3 collective-permute-start
  10.4 0.0 all-gather.3.cloned.1.call-update
  10.4 0.0 reduce-scatter.4.cloned.1.call-start
  10.5 0.0 copy-done.10
  10.5 0.7 fusion.26
  11.2 0.0 copy-done
  11.2 0.0 copy-start.9
  11.2 0.7 fusion.9
  11.9 0.1 copy-done.9
  12.0 0.7 fusion.1
  12.8 0.0 copy-start.13
  12.8 0.7 convolution_add_fusion.2
  13.5 0.0 copy-start.2
  13.6 0.0 copy-start.12
  13.6 23.0 %collective-permute-done = bf16[128,4096]{1,0:T(8,128)(2,1)S(1)} collective-permute-done((bf16[128,4096]{1,0:T(8,128)(2,1)S(1)}, bf16[128,4096]{1,0:T(8,128)(2,1)S(1)}, u32[]{:S(2)}, u32[]{:S(2)}) %collective-permute-start) | collective-permute-done | bytes 1048608 | tf_op jit(solution)/shard_map/ppermute | solution.py:36
  36.6 0.0 copy-done.13
  36.6 0.7 fusion.27
  37.3 0.0 copy-done.12
  37.3 0.7 fusion
  38.0 0.0 copy-done.2
  38.0 3.2 %multiply_add_fusion = (f32[128,4096]{1,0:T(8,128)}, f32[128,4096]{1,0:T(8,128)}, f32[128,4096]{1,0:T(8,128)}) fusion(f32[256,4096]{1,0:T(8,128)S(1)} %convolution_add_fusion.2, f32[256,4096]{1,0:T(8,128)S(1)} %fusion, f32[256,4096]{1,0:T(8,128)S(1)} %fusion.1), kind=kLoop, calls=%fused_computation.22 | loop fusion | flops 2621440 | bytes 18874368 | tf_op jit(solution)/shard_map/add | solution.py:54
  41.2 11.1 %all-gather.3.cloned.1.call-done = bf16[128,4096]{1,0:T(8,128)(2,1)} async-done(((bf16[8,4096]{1,0:T(8,128)(2,1)}), bf16[128,4096]{1,0:T(8,128)(2,1)}) %all-gather.3.cloned.1.call-update) | async-done | bytes 1048592 | tf_op jit(solution)/shard_map/all_gather | solution.py:37
  52.4 0.0 copy-start.7
  52.4 2.0 %fusion.25 = f32[256,4096]{1,0:T(8,128)S(1)} fusion(bf16[256,128]{1,0:T(8,128)(2,1)S(1)} %copy-done.10, bf16[128,4096]{1,0:T(8,128)(2,1)} %all-gather.3.cloned.1.call-done), kind=kOutput, calls=%fused_computation.40 | convolution fusion | flops 268435456 | bytes 5308416 | tf_op jit(solution)/shard_map/dot_general | solution.py:23
  54.4 0.0 copy-done.7
  54.4 0.0 copy-start.3
  54.4 0.0 copy-start.6
  54.4 0.7 convolution_add_fusion.3
  55.2 1.4 %copy-done.3 = f32[256,4096]{1,0:T(8,128)S(1)} copy-done((f32[256,4096]{1,0:T(8,128)S(1)}, f32[256,4096]{1,0:T(8,128)}, u32[]{:S(2)}) %copy-start.3) | copy-done | bytes 4194328
  56.6 0.7 copy-done.6
  57.3 0.0 copy-start.5
  57.3 0.0 copy-start.8
  57.3 4.2 %multiply_add_fusion.1 = (f32[128,4096]{1,0:T(8,128)S(1)}, f32[128,4096]{1,0:T(8,128)}, f32[128,4096]{1,0:T(8,128)S(1)}) fusion(f32[128,4096]{1,0:T(8,128)S(1)} %copy-done.6, f32[128,4096]{1,0:T(8,128)} %get-tuple-element.10, f32[256,4096]{1,0:T(8,128)S(1)} %convolution_add_fusion.3, f32[256,4096]{1,0:T(8,128)S(1)} %copy-done.3), kind=kLoop, calls=%fused_computation.24 | loop fusion | flops 4718592 | bytes 18874368 | tf_op jit(solution)/shard_map/add | solution.py:56
  61.5 0.0 copy-done.5
  61.5 0.0 copy-done.8
  61.5 0.0 copy-start.11
  61.5 0.8 fusion.17
  62.3 0.1 copy-done.11
  62.3 0.8 convolution_add_fusion.5
  63.1 2.1 %fusion.2 = f32[128,4096]{0,1:T(8,128)} fusion(f32[4096,128]{1,0:T(8,128)S(1)} %convolution_add_fusion.5, bf16[128,256]{1,0:T(8,128)(2,1)S(1)} %copy-done.8, f32[128,4096]{1,0:T(8,128)S(1)} %get-tuple-element.13, f32[128,4096]{1,0:T(8,128)S(1)} %copy-done.5), kind=kOutput, calls=%fused_computation.7 | convolution fusion | flops 274202624 | bytes 8454144 | tf_op jit(solution)/shard_map/dot_general | solution.py:23
  65.2 2.9 %copy.25 = f32[128,4096]{1,0:T(8,128)} copy(f32[128,4096]{0,1:T(8,128)} %fusion.2) | data formatting | bytes 4194304
  68.2 0.0 reduce-scatter.4.cloned.1.call-update
  68.2 0.0 copy-start.4
  68.2 2.5 %fusion.13 = f32[4096,128]{1,0:T(8,128)S(1)} fusion(bf16[128,256]{1,0:T(8,128)(2,1)S(1)} %copy-done.8, f32[128,4096]{1,0:T(8,128)} %get-tuple-element.12, f32[128,4096]{1,0:T(8,128)S(1)} %get-tuple-element.11), kind=kOutput, calls=%fused_computation.30 | convolution fusion | flops 272629760 | bytes 6356992 | tf_op jit(solution)/shard_map/dot_general | solution.py:23
  70.7 0.0 copy-done.4
  70.7 0.8 convolution_add_fusion.7
  71.5 0.0 copy-start.1
  71.5 1.8 %fusion.4 = bf16[1,128,4096]{1,2,0:T(8,128)(2,1)} fusion(f32[4096,128]{1,0:T(8,128)S(1)} %convolution_add_fusion.7, bf16[128,256]{1,0:T(8,128)(2,1)S(1)} %copy-done.8, f32[128,4096]{1,0:T(8,128)S(1)} %copy-done.4, f32[128,4096]{1,0:T(8,128)S(1)} %get-tuple-element.11), kind=kOutput, calls=%fused_computation.12 | convolution fusion | flops 274726912 | bytes 7405568 | tf_op jit(solution)/shard_map/dot_general | solution.py:23
  73.3 2.3 %copy.24 = bf16[1,128,4096]{2,1,0:T(8,128)(2,1)} copy(bf16[1,128,4096]{1,2,0:T(8,128)(2,1)} %fusion.4) | data formatting | bytes 2097152
  75.6 53.6 %reduce-scatter.4.cloned.1.call-done = f32[8,4096]{1,0:T(8,128)} async-done(((f32[128,4096]{1,0:T(8,128)}), f32[8,4096]{1,0:T(8,128)}) %reduce-scatter.4.cloned.1.call-update) | async-done | bytes 131088 | tf_op jit(solution)/shard_map/reduce_scatter | solution.py:58
  129.1 5.8 %all-gather = f32[16,4096]{1,0:T(8,128)S(1)} all-gather(f32[8,4096]{1,0:T(8,128)} %reduce-scatter.4.cloned.1.call-done), channel_id=2, replica_groups=mesh['dp'=16,'ctx'=2] {'ctx'}, dimensions={0}, use_global_device_ids=true | all-gather | bytes 393216 | tf_op jit(solution)/shard_map/all_gather | solution.py:58
  135.0 0.7 broadcast_multiply_fusion
  135.6 0.0 copy-done.1
  (1 shorter events, 0.0 us)
Async XLA Ops:
  7.2 4.0 %copy-start = (bf16[1,128,4096]{2,1,0:T(8,128)(2,1)S(1)}, bf16[1,128,4096]{2,1,0:T(8,128)(2,1)}, u32[]{:S(2)}) copy-start(bf16[1,128,4096]{2,1,0:T(8,128)(2,1)} %param.18) | copy-start | bytes 3145732
  7.2 3.3 %copy-start.10 = (bf16[256,128]{1,0:T(8,128)(2,1)S(1)}, bf16[256,128]{1,0:T(8,128)(2,1)}, u32[]{:S(2)}) copy-start(bf16[256,128]{1,0:T(8,128)(2,1)} %constant.16.clone) | copy-start | bytes 196612
  7.2 45.2 %all-gather.3.cloned.1.call-start = ((), (), s32[]{:S(2)}) async-start(), calls=%async_computation.1 | async-start | bytes 1114112 | tf_op jit(solution)/shard_map/all_gather | solution.py:37
  9.1 27.5 %collective-permute-start = (bf16[128,4096]{1,0:T(8,128)(2,1)S(1)}, bf16[128,4096]{1,0:T(8,128)(2,1)S(1)}, u32[]{:S(2)}, u32[]{:S(2)}) collective-permute-start(bf16[128,4096]{1,0:T(8,128)(2,1)S(1)} %fusion.7), channel_id=1, source_target_pairs={{1,0},{3,2},{5,4},{7,6},{9,8},{11,10},{13,12},{15,14},{17,16},{19,... | collective-permute-start | bytes 3145736 | tf_op jit(solution)/shard_map/ppermute | solution.py:36
  10.4 118.7 %reduce-scatter.4.cloned.1.call-start = ((), (), s32[]{:S(2)}) async-start(), calls=%async_computation.2 | async-start | bytes 2228224 | tf_op jit(solution)/shard_map/reduce_scatter | solution.py:58
  11.2 0.8 copy-start.9
  12.8 23.8 %copy-start.13 = (bf16[256,128]{1,0:T(8,128)(2,1)S(1)}, bf16[256,128]{1,0:T(8,128)(2,1)}, u32[]{:S(2)}) copy-start(bf16[256,128]{1,0:T(8,128)(2,1)} %constant.19.clone) | copy-start | bytes 196612
  13.5 24.5 %copy-start.2 = (f32[256,4096]{1,0:T(8,128)}, f32[256,4096]{1,0:T(8,128)S(1)}, u32[]{:S(2)}) copy-start(f32[256,4096]{1,0:T(8,128)S(1)} %convolution_add_fusion.2) | copy-start | bytes 12582916
  13.6 23.7 %copy-start.12 = (bf16[256,128]{1,0:T(8,128)(2,1)S(1)}, bf16[256,128]{1,0:T(8,128)(2,1)}, u32[]{:S(2)}) copy-start(bf16[256,128]{1,0:T(8,128)(2,1)} %constant.18.clone) | copy-start | bytes 196612
  52.4 2.0 %copy-start.7 = (bf16[128,4096]{1,0:T(8,128)(2,1)S(1)}, bf16[128,4096]{1,0:T(8,128)(2,1)}, u32[]{:S(2)}) copy-start(bf16[128,4096]{1,0:T(8,128)(2,1)} %all-gather.3.cloned.1.call-done) | copy-start | bytes 3145732
  54.4 2.2 %copy-start.3 = (f32[256,4096]{1,0:T(8,128)S(1)}, f32[256,4096]{1,0:T(8,128)}, u32[]{:S(2)}) copy-start(f32[256,4096]{1,0:T(8,128)} %copy-done.2) | copy-start | bytes 12582916
  54.4 2.9 %copy-start.6 = (f32[128,4096]{1,0:T(8,128)S(1)}, f32[128,4096]{1,0:T(8,128)}, u32[]{:S(2)}) copy-start(f32[128,4096]{1,0:T(8,128)} %get-tuple-element.9) | copy-start | bytes 6291460
  57.3 4.2 %copy-start.5 = (f32[128,4096]{1,0:T(8,128)S(1)}, f32[128,4096]{1,0:T(8,128)}, u32[]{:S(2)}) copy-start(f32[128,4096]{1,0:T(8,128)} %get-tuple-element.8) | copy-start | bytes 6291460
  57.3 4.2 %copy-start.8 = (bf16[128,256]{1,0:T(8,128)(2,1)S(1)}, bf16[128,256]{1,0:T(8,128)(2,1)}, u32[]{:S(2)}) copy-start(bf16[128,256]{1,0:T(8,128)(2,1)} %constant.20.clone) | copy-start | bytes 196612
  61.5 0.8 copy-start.11
  68.2 2.5 %copy-start.4 = (f32[128,4096]{1,0:T(8,128)S(1)}, f32[128,4096]{1,0:T(8,128)}, u32[]{:S(2)}) copy-start(f32[128,4096]{1,0:T(8,128)} %get-tuple-element.12) | copy-start | bytes 6291460
  71.5 64.1 %copy-start.1 = (bf16[1,128,4096]{2,1,0:T(8,128)(2,1)S(1)}, bf16[1,128,4096]{2,1,0:T(8,128)(2,1)}, u32[]{:S(2)}) copy-start(bf16[1,128,4096]{2,1,0:T(8,128)(2,1)} %param.18) | copy-start | bytes 3145732
Sparse Core Ops, SparseCore 0:
  10.6 41.7 all-gather.2
  68.3 60.7 reduce-scatter.3
